TPU v7x, 256 devices: a whole 4x4x8 slice. The times are simulated.
256 devices in a mesh: snap: 64 (over x, y, z_hi), feat: 4 (over z_lo, core).
Axes of the slice: x: 4, y: 4, z: 8 (z_hi: 4, z_lo: 2; z = z_hi * 2 + z_lo), core: 2. Of those that a mesh axis runs over, the one named last changes fastest.
Arguments:
- features: bfloat16 [64, 2048, 1024], P('snap', None, 'feat'), may hold values from -6 to 6
- block_index: int32 [64, 16, 8], P('snap'), may hold values from 0 to 15
- block_values: bfloat16 [64, 16, 8, 128, 128], P('snap'), may hold values from -0.1875 to 0.1875
- hop_in: bfloat16 [1024, 1024], P(None, 'feat'), may hold values from -0.1875 to 0.1875
- query_w: bfloat16 [1024, 1024], P(None, 'feat'), may hold values from -0.1875 to 0.1875
- key_w: bfloat16 [1024, 1024], P(None, 'feat'), may hold values from -0.1875 to 0.1875
- value_w: bfloat16 [1024, 1024], P(None, 'feat'), may hold values from -0.1875 to 0.1875
- output_w: bfloat16 [1024, 1024], P(None, 'feat'), may hold values from -0.1875 to 0.1875
- hop_out: bfloat16 [1024, 1024], P(None, 'feat'), may hold values from -0.1875 to 0.1875
- time_bias: float32 [64, 64], replicated, may hold values from -2 to 403
Outputs:
- result: bfloat16 [64, 2048, 1024], P('snap', None, 'feat')
All inputs are finite; a program needn't handle non-finite values.
Results may differ from a plain program's by a relative error of at most 0.012.
Values may be sent and summed in bfloat16 or wider, within the bound.
No kernel may reach another device: no remote copies, remote signals or barrier semaphores. Data moves between devices by JAX's collectives and lax.ppermute only.
A program may use at most 64 MiB of HBM per device.

v0:
```python
import math
import jax
import jax.numpy as jnp
from jax import lax
from jax.sharding import PartitionSpec as P


def sent_to_all(shard, axis):
    copies = jnp.broadcast_to(shard, (lax.axis_size(axis), *shard.shape))
    return lax.all_to_all(copies, axis, split_axis=0, concat_axis=0, tiled=True)


def over_copies(shard, axis):
    everything = sent_to_all(shard, axis)
    return jnp.sum(everything.astype(jnp.float32), axis=0)


def aggregate(field, block_index, block_values):
    count_snap, vertices, columns = field.shape
    rows_blk = block_values.shape[-1]
    blocks = field.reshape(count_snap, vertices // rows_blk, rows_blk, columns)
    picked = jax.vmap(lambda plane, index_row: plane[index_row])(blocks, block_index)
    summed = jnp.einsum(
        "srkij,srkjc->sric", block_values, picked, preferred_element_type=jnp.float32
    )
    return summed.reshape(count_snap, vertices, columns).astype(jnp.bfloat16)


def add_rows(piece, weight):
    return jnp.einsum("svc,cd->svd", piece, weight, preferred_element_type=jnp.float32)


def attend(scores, values, time_bias, score_scale):
    logits = scores * score_scale + time_bias[None]
    shifted = logits - jnp.max(logits, axis=2, keepdims=True)
    weights = jnp.exp(shifted)
    probs = (weights / jnp.sum(weights, axis=2, keepdims=True)).astype(jnp.bfloat16)
    return jnp.einsum("uts,suc->tuc", probs, values, preferred_element_type=jnp.float32).astype(
        jnp.bfloat16
    )


def local(
    features,
    block_index,
    block_values,
    hop_in,
    query_w,
    key_w,
    value_w,
    output_w,
    hop_out,
    time_bias,
):
    score_scale = 1.0 / math.sqrt(query_w.shape[0])
    agg_first = aggregate(features, block_index, block_values)
    lifted = add_rows(lax.all_gather(agg_first, "feat", axis=2, tiled=True), hop_in)
    hidden = jax.nn.relu(lifted).astype(jnp.bfloat16)
    owned_hidden = lax.all_to_all(hidden, "snap", split_axis=1, concat_axis=0, tiled=True)
    piece = lax.all_gather(owned_hidden, "feat", axis=2, tiled=True)
    query_sum = add_rows(piece, query_w)
    keys_sum = add_rows(piece, key_w)
    values_sum = add_rows(piece, value_w)
    query_part = query_sum.astype(jnp.bfloat16)
    keys_part = keys_sum.astype(jnp.bfloat16)
    values_part = values_sum.astype(jnp.bfloat16)
    query_own, keys_own, values_own = (query_part, keys_part, values_part)
    partial_scores = jnp.einsum(
        "tuc,suc->uts", query_own, keys_own, preferred_element_type=jnp.float32
    )
    scores = over_copies(partial_scores.astype(jnp.bfloat16), "feat").astype(jnp.float32)
    context = attend(scores, values_own, time_bias, score_scale)
    gathered = lax.all_to_all(context, "snap", split_axis=0, concat_axis=1, tiled=True)
    update = add_rows(lax.all_gather(gathered, "feat", axis=2, tiled=True), output_w)
    mixed = (hidden.astype(jnp.float32) + update).astype(jnp.bfloat16)
    agg_second = aggregate(mixed, block_index, block_values)
    final_sum = add_rows(lax.all_gather(agg_second, "feat", axis=2, tiled=True), hop_out)
    return jax.nn.relu(final_sum).astype(jnp.bfloat16)


def solution(mesh):
    in_specs = (
        P("snap", None, "feat"),
        P("snap", None, None),
        P("snap", None, None, None, None),
        P(None, "feat"),
        P(None, "feat"),
        P(None, "feat"),
        P(None, "feat"),
        P(None, "feat"),
        P(None, "feat"),
        P(),
    )
    out_specs = P("snap", None, "feat")
    return jax.shard_map(local, mesh=mesh, in_specs=in_specs, out_specs=out_specs, check_vma=False)
```

profile of v0, /device:TPU:1, one launch (start us, length us, event | category | flops | bytes accessed | tf_op | source)
XLA Modules:
  0.0 392.6 jit_solution(9581406341102095699)
XLA Ops:
  6.5 0.8 fusion.52
  7.8 6.7 %gather_fusion = bf16[128,128,256]{2,1,0:T(8,128)(2,1)} fusion(bf16[1,16,128,256]{3,2,1,0:T(8,128)(2,1)S(1)} %bitcast.85, s32[128]{0:T(128)S(1)} %reshape.87), kind=kCustom, calls=%fused_computation | custom fusion | bytes 16778240 | tf_op jit(solution)/shard_map/vmap()/gather | solution.py:22
  14.5 7.2 %bitcast_convert_fusion.1 = bf16[16,256,128]{1,2,0:T(8,128)(2,1)} fusion(bf16[16,8,128,256]{3,2,1,0:T(8,128)(2,1)} %bitcast.88, bf16[1,16,8,128,128]{4,3,2,1,0:T(8,128)(2,1)} %param.12), kind=kOutput, calls=%fused_computation.22 | convolution fusion | flops 1074266112 | bytes 13631488 | tf_op jit(solution)/shard_map/srkij,srkjc->sric/dot_general | solution.py:23
  21.8 53.4 %all-gather.5.cloned.1.call-done = bf16[1,2048,1024]{2,1,0:T(8,128)(2,1)} async-done(((bf16[1,2048,256]{2,1,0:T(8,128)(2,1)}), bf16[1,2048,1024]{2,1,0:T(8,128)(2,1)}) %all-gather.5.cloned.1.call-update) | async-done | bytes 4194320 | tf_op jit(solution)/shard_map/all_gather | solution.py:57
  75.1 3.4 fusion.26
  78.6 11.7 %copy.29 = bf16[1,2048,256]{2,0,1:T(2,128)(2,1)S(1)} copy(bf16[1,2048,256]{2,1,0:T(8,128)(2,1)S(1)} %bitcast.95) | data formatting | bytes 2097152 | tf_op jit(solution)/shard_map/convert_element_type | solution.py:58
  90.9 10.6 %reduce = bf16[2048,256]{1,0:T(8,128)(2,1)S(1)} reduce(bf16[2048,1,256]{2,1,0:T(2,128)(2,1)S(1)} %bitcast.90, bf16[]{:T(256)} %broadcast.44), dimensions={1}, to_apply=%bitcast.84.reduce_sub_computation | reduce | bytes 2097154
  101.8 39.5 %all_to_all.29 = bf16[64,2,4096]{2,1,0:T(2,128)(2,1)S(1)} all-to-all(bf16[64,2,4096]{2,1,0:T(2,128)(2,1)S(1)} %reshape.110), channel_id=1, replica_groups=mesh['snap'=64,'feat'=4] {'snap'}, dimensions={0} | all-to-all | bytes 2097152 | tf_op jit(solution)/shard_map/all_to_all | solution.py:59
  141.3 1.0 reshape.111
  142.6 1.6 copy.23
  144.4 46.8 %all-gather.7.cloned.1.call-done = bf16[64,32,1024]{2,0,1:T(8,128)(2,1)} async-done(((bf16[64,32,256]{2,0,1:T(8,128)(2,1)}), bf16[64,32,1024]{2,0,1:T(8,128)(2,1)}) %all-gather.7.cloned.1.call-update) | async-done | bytes 4194320 | tf_op jit(solution)/shard_map/all_gather | solution.py:60
  191.2 3.6 convolution_convert_fusion
  194.8 3.9 fusion.42
  199.2 1.7 reshape.112
  200.9 16.1 %all_to_all.30 = bf16[4,2,65536]{2,1,0:T(2,128)(2,1)} all-to-all(bf16[4,2,65536]{2,1,0:T(2,128)(2,1)S(1)} %reshape.112), channel_id=1, replica_groups=mesh['snap'=64,'feat'=4] {'feat'}, dimensions={0} | all-to-all | bytes 2097152 | tf_op jit(solution)/shard_map/all_to_all | solution.py:10
  217.0 3.1 reshape.113
  221.2 6.0 %fusion.39 = bf16[64,32,256]{2,0,1:T(8,128)(2,1)S(1)} fusion(bf16[64,32,1024]{2,0,1:T(8,128)(2,1)} %all-gather.7.cloned.1.call-done, bf16[1024,256]{1,0:T(8,128)(2,1)} %param.16, f32[32,64]{1,0:T(8,128)S(1)} %fusion.60, f32[32,64,64]{2,1,0:T(8,128)S(1)} %convert_reduce_fusion, f32[64,64]{1,0:T(8,128)S(1)} %copy-done.7), kind=kOutput, calls=%fused_computation.29 | convolution fusion | flops 1142556672 | bytes 6316032 | tf_op jit(solution)/shard_map/uts,suc->tuc/dot_general | solution.py:38
  227.8 41.7 %all_to_all.31 = bf16[64,32,256]{2,1,0:T(8,128)(2,1)} all-to-all(bf16[64,32,256]{2,1,0:T(8,128)(2,1)S(1)} %copy.24), channel_id=1, replica_groups=mesh['snap'=64,'feat'=4] {'snap'}, dimensions={0} | all-to-all | bytes 2097152 | tf_op jit(solution)/shard_map/all_to_all | solution.py:73
  269.8 44.8 %all-gather.9.cloned.1.call-done = bf16[1,2048,1024]{2,1,0:T(8,128)(2,1)} async-done(((bf16[1,2048,256]{2,1,0:T(8,128)(2,1)}), bf16[1,2048,1024]{2,1,0:T(8,128)(2,1)}) %all-gather.9.cloned.1.call-update) | async-done | bytes 4194320 | tf_op jit(solution)/shard_map/all_gather | solution.py:74
  314.6 3.6 fusion.20
  318.2 6.7 %gather_fusion.1 = bf16[128,128,256]{2,1,0:T(8,128)(2,1)} fusion(bf16[1,16,128,256]{3,2,1,0:T(8,128)(2,1)S(1)} %bitcast.86, s32[128]{0:T(128)S(1)} %reshape.87), kind=kCustom, calls=%fused_computation.1 | custom fusion | bytes 16778240 | tf_op jit(solution)/shard_map/vmap()/gather | solution.py:22
  324.9 7.2 %bitcast_convert_fusion = bf16[16,256,128]{1,2,0:T(8,128)(2,1)} fusion(bf16[16,8,128,256]{3,2,1,0:T(8,128)(2,1)} %bitcast.87, bf16[1,16,8,128,128]{4,3,2,1,0:T(8,128)(2,1)} %param.12), kind=kOutput, calls=%fused_computation.21 | convolution fusion | flops 1074266112 | bytes 13631488 | tf_op jit(solution)/shard_map/srkij,srkjc->sric/dot_general | solution.py:23
  332.2 49.5 %all-gather.11.cloned.1.call-done = bf16[1,2048,1024]{2,1,0:T(8,128)(2,1)} async-done(((bf16[1,2048,256]{2,1,0:T(8,128)(2,1)}), bf16[1,2048,1024]{2,1,0:T(8,128)(2,1)}) %all-gather.11.cloned.1.call-update) | async-done | bytes 4194320 | tf_op jit(solution)/shard_map/all_gather | solution.py:77
  381.7 4.4 %fusion.29 = bf16[1,2048,256]{2,1,0:T(8,128)(2,1)} fusion(bf16[1024,256]{1,0:T(8,128)(2,1)S(1)} %copy-done.6, bf16[1,2048,1024]{2,1,0:T(8,128)(2,1)} %all-gather.11.cloned.1.call-done), kind=kOutput, calls=%fused_computation.20 | convolution fusion | flops 1074790400 | bytes 5767168 | tf_op jit(solution)/shard_map/svc,cd->svd/dot_general | solution.py:30
  (35 shorter events, 4.3 us)
Async XLA Ops:
  6.5 1.2 copy-start
  6.5 68.6 %all-gather.5.cloned.1.call-start = ((), (), s32[]{:S(2)}) async-start(), calls=%async_computation.3 | async-start | bytes 5242880 | tf_op jit(solution)/shard_map/all_gather | solution.py:57
  14.5 60.7 %copy-start.4 = (bf16[1024,256]{1,0:T(8,128)(2,1)S(1)}, bf16[1024,256]{1,0:T(8,128)(2,1)}, u32[]{:S(2)}) copy-start(bf16[1024,256]{1,0:T(8,128)(2,1)} %param.13) | copy-start | bytes 1572868
  21.7 169.5 %all-gather.7.cloned.1.call-start = ((), (), s32[]{:S(2)}) async-start(), calls=%async_computation.4 | async-start | bytes 5242880 | tf_op jit(solution)/shard_map/all_gather | solution.py:60
  78.6 11.8 %copy-start.2 = (bf16[2048,256]{1,0:T(8,128)(2,1)}, bf16[2048,256]{1,0:T(8,128)(2,1)S(1)}, u32[]{:S(2)}) copy-start(bf16[2048,256]{1,0:T(8,128)(2,1)S(1)} %fusion.26) | copy-start | bytes 3145732
  144.1 50.6 %copy-start.5 = (bf16[1024,256]{1,0:T(8,128)(2,1)S(1)}, bf16[1024,256]{1,0:T(8,128)(2,1)}, u32[]{:S(2)}) copy-start(bf16[1024,256]{1,0:T(8,128)(2,1)} %param.14) | copy-start | bytes 1572868
  144.2 170.5 %all-gather.9.cloned.1.call-start = ((), (), s32[]{:S(2)}) async-start(), calls=%async_computation.5 | async-start | bytes 5242880 | tf_op jit(solution)/shard_map/all_gather | solution.py:74
  200.9 19.6 %copy-start.7 = (f32[64,64]{1,0:T(8,128)S(1)}, f32[64,64]{1,0:T(8,128)}, u32[]{:S(2)}) copy-start(f32[64,64]{1,0:T(8,128)} %param.19) | copy-start | bytes 49156
  227.2 87.4 %copy-start.3 = (bf16[2048,256]{1,0:T(8,128)(2,1)S(1)}, bf16[2048,256]{1,0:T(8,128)(2,1)}, u32[]{:S(2)}) copy-start(bf16[2048,256]{1,0:T(8,128)(2,1)} %copy-done.2) | copy-start | bytes 3145732
  269.6 112.1 %all-gather.11.cloned.1.call-start = ((), (), s32[]{:S(2)}) async-start(), calls=%async_computation.6 | async-start | bytes 5242880 | tf_op jit(solution)/shard_map/all_gather | solution.py:77
  324.9 56.7 %copy-start.6 = (bf16[1024,256]{1,0:T(8,128)(2,1)S(1)}, bf16[1024,256]{1,0:T(8,128)(2,1)}, u32[]{:S(2)}) copy-start(bf16[1024,256]{1,0:T(8,128)(2,1)} %param.18) | copy-start | bytes 1572868
  332.2 53.9 %copy-start.1 = (bf16[1,2048,256]{2,1,0:T(8,128)(2,1)S(1)}, bf16[1,2048,256]{2,1,0:T(8,128)(2,1)}, u32[]{:S(2)}) copy-start(bf16[1,2048,256]{2,1,0:T(8,128)(2,1)} %param.10) | copy-start | bytes 3145732
Sparse Core Ops, SparseCore 0:
  21.8 53.2 all-gather.4
  144.3 46.8 all-gather.6
  269.7 44.8 all-gather.8
  332.3 49.3 all-gather.10
where the time goes:
time: 393 us
  waiting for transfers between devices  195 us (50%)
  blocking collectives  97.3 us (25%)
  matrix products  39.3 us (10%)
  local copies, waits for them, and re-layouts  35.2 us (9%)
  between operations  13.3 us (3%)
  other arithmetic  12.4 us (3%)
    all_gather x1, waiting for transfers between devices, local(): lax.all_gather(agg_first, 'feat', axis=2, tiled=True)  53.4 us
    all_gather x1, waiting for transfers between devices, local(): lax.all_gather(agg_second, 'feat', axis=2, tiled=True)  49.5 us
    all_gather x1, waiting for transfers between devices, local(): piece = lax.all_gather(owned_hidden, 'feat', axis=2, tiled=True)  46.8 us
    all_gather x1, waiting for transfers between devices, local(): lax.all_gather(gathered, 'feat', axis=2, tiled=True)  44.8 us
    all_to_all x1, blocking collectives, local(): lax.all_to_all(context, 'snap', split_axis=0, concat_axis=1, tiled=True)  41.7 us
    all_to_all x1, blocking collectives, local(): lax.all_to_all(hidden, 'snap', split_axis=1, concat_axis=0, tiled=True)  39.5 us
    all_to_all x1, blocking collectives, sent_to_all(): return lax.all_to_all(copies, axis, split_axis=0, concat_axis=0, tiled=True)  16.1 us
    dot_general x4, matrix products, add_rows(): jnp.einsum('svc,cd->svd', piece, weight, preferred_element_type=jnp.float32)  15 us
  transfers between devices with their start and end apart: 4, of which 4 were waited for; matrix products, arithmetic and copies ran while one was open for 0% of the time, Pallas kernels for 0%

commit v1 on v0

--- a/solution.py
+++ b/solution.py
@@ -56,7 +56,10 @@
     agg_first = aggregate(features, block_index, block_values)
     lifted = add_rows(lax.all_gather(agg_first, "feat", axis=2, tiled=True), hop_in)
     hidden = jax.nn.relu(lifted).astype(jnp.bfloat16)
-    owned_hidden = lax.all_to_all(hidden, "snap", split_axis=1, concat_axis=0, tiled=True)
+    owned_hidden = jnp.concatenate(
+        lax.all_to_all(jnp.stack(jnp.split(hidden, lax.axis_size("snap"), axis=1)), "snap", 0, 0),
+        axis=0,
+    )
     piece = lax.all_gather(owned_hidden, "feat", axis=2, tiled=True)
     query_sum = add_rows(piece, query_w)
     keys_sum = add_rows(piece, key_w)

time: 393 us -> 383 us (0.975)
  local copies, waits for them, and re-layouts: 35.2 us -> 23.2 us
  other arithmetic: 12.4 us -> 1.84 us
  matrix products: 39.3 us -> 49.6 us
    convert_element_type x1 -> x0, local copies, waits for them, and re-layouts: 11.7 us -> none  [local(): hidden = jax.nn.relu(lifted).astype(jnp.bfloat16)]
    unnamed x1 -> x0, other arithmetic: 10.6 us -> none
where the time goes in v1:
time: 383 us; the launch traced here: 382 us
  waiting for transfers between devices  194 us (51%)
  blocking collectives  99.5 us (26%)
  matrix products  49.6 us (13%)
  local copies, waits for them, and re-layouts  23.2 us (6%)
  between operations  13.7 us (4%)
    all_gather x1, waiting for transfers between devices, local(): lax.all_gather(agg_first, 'feat', axis=2, tiled=True)  53.4 us
    all_gather x1, waiting for transfers between devices, local(): lax.all_gather(agg_second, 'feat', axis=2, tiled=True)  49.5 us
    all_gather x1, waiting for transfers between devices, local(): piece = lax.all_gather(owned_hidden, 'feat', axis=2, tiled=True)  46.8 us
    all_gather x1, waiting for transfers between devices, local(): lax.all_gather(gathered, 'feat', axis=2, tiled=True)  44.2 us
    all_to_all x1, blocking collectives, local(): lax.all_to_all(context, 'snap', split_axis=0, concat_axis=1, tiled=True)  42.5 us
    all_to_all x1, blocking collectives, local(): lax.all_to_all(jnp.stack(jnp.split(hidden, lax.axis_size('snap'), axis=1)...  39.6 us
    dot_general x4, matrix products, add_rows(): jnp.einsum('svc,cd->svd', piece, weight, preferred_element_type=jnp.float32)  18.4 us
    all_to_all x1, blocking collectives, sent_to_all(): return lax.all_to_all(copies, axis, split_axis=0, concat_axis=0, tiled=True)  17.4 us
  transfers between devices with their start and end apart: 4, of which 4 were waited for; matrix products, arithmetic and copies ran while one was open for 0% of the time, Pallas kernels for 0%

profile of v1, /device:TPU:1, one launch (start us, length us, event | category | flops | bytes accessed | tf_op | source)
XLA Modules:
  0.0 382.4 jit_solution(4764038277613881215)
XLA Ops:
  6.5 0.8 fusion.77
  7.8 6.7 %gather_fusion = bf16[128,128,256]{2,1,0:T(8,128)(2,1)} fusion(bf16[1,16,128,256]{3,2,1,0:T(8,128)(2,1)S(1)} %bitcast.334, s32[128]{0:T(128)S(1)} %reshape.88), kind=kCustom, calls=%fused_computation | custom fusion | bytes 16778240 | tf_op jit(solution)/shard_map/vmap()/gather | solution.py:22
  14.5 7.2 %bitcast_convert_fusion.1 = bf16[16,256,128]{1,2,0:T(8,128)(2,1)} fusion(bf16[16,8,128,256]{3,2,1,0:T(8,128)(2,1)} %bitcast.337, bf16[1,16,8,128,128]{4,3,2,1,0:T(8,128)(2,1)} %param.12), kind=kOutput, calls=%fused_computation.28 | convolution fusion | flops 1074266112 | bytes 13631488 | tf_op jit(solution)/shard_map/srkij,srkjc->sric/dot_general | solution.py:23
  21.8 53.4 %all-gather.6.cloned.1.call-done = bf16[1,2048,1024]{2,1,0:T(8,128)(2,1)} async-done(((bf16[1,2048,256]{2,1,0:T(8,128)(2,1)}), bf16[1,2048,1024]{2,1,0:T(8,128)(2,1)}) %all-gather.6.cloned.1.call-update) | async-done | bytes 4194320 | tf_op jit(solution)/shard_map/all_gather | solution.py:57
  75.1 3.4 fusion.32
  79.5 39.6 %all_to_all.22 = bf16[64,1,32,256]{3,2,1,0:T(8,128)(2,1)} all-to-all(bf16[64,1,32,256]{3,2,1,0:T(8,128)(2,1)S(1)} %constant_dynamic-update-slice_fusion), channel_id=1, replica_groups=mesh['snap'=64,'feat'=4] {'snap'}, dimensions={0} | all-to-all | bytes 2097152 | tf_op jit(solution)/shard_map/all_to_all | solution.py:60
  119.4 46.8 %all-gather.12.cloned.1.call-done = bf16[64,1,32,1024]{3,2,1,0:T(8,128)(2,1)} async-done(((bf16[64,1,32,256]{3,2,1,0:T(8,128)(2,1)}), bf16[64,1,32,1024]{3,2,1,0:T(8,128)(2,1)}) %all-gather.12.cloned.1.call-update) | async-done | bytes 4194320 | tf_op jit(solution)/shard_map/all_gather | solution.py:63
  166.3 7.0 %fusion.51 = bf16[64,32,256]{2,0,1:T(8,128)(2,1)S(1)} fusion(bf16[64,32,1024]{2,1,0:T(8,128)(2,1)} %bitcast.405, bf16[1024,256]{1,0:T(8,128)(2,1)S(1)} %copy-done.5), kind=kOutput, calls=%fused_computation.32 | convolution fusion | flops 1074266112 | bytes 5767168 | tf_op jit(solution)/shard_map/svc,cd->svd/dot_general | solution.py:30
  173.2 7.6 %fusion.65 = bf16[32,64,64]{2,1,0:T(8,128)(2,1)} fusion(bf16[64,32,256]{2,0,1:T(8,128)(2,1)S(1)} %fusion.51, bf16[64,32,1024]{2,1,0:T(8,128)(2,1)} %bitcast.406, bf16[1024,256]{1,0:T(8,128)(2,1)S(1)} %copy-done.6), kind=kOutput, calls=%fused_computation.38 | convolution fusion | flops 1141506048 | bytes 6029312 | tf_op jit(solution)/shard_map/tuc,suc->uts/dot_general | solution.py:71
  180.8 1.6 broadcast_in_dim.5
  182.4 2.7 reshape.112
  185.1 17.4 %all_to_all.23 = bf16[4,2,65536]{2,1,0:T(2,128)(2,1)} all-to-all(bf16[4,2,65536]{2,1,0:T(2,128)(2,1)} %reshape.112), channel_id=1, replica_groups=mesh['snap'=64,'feat'=4] {'feat'}, dimensions={0} | all-to-all | bytes 2097152 | tf_op jit(solution)/shard_map/all_to_all | solution.py:10
  202.5 3.1 reshape.113
  206.0 1.0 copy-done.1
  207.0 0.6 fusion.85
  207.6 9.1 %fusion.59 = bf16[64,32,256]{2,0,1:T(8,128)(2,1)S(1)} fusion(bf16[64,32,1024]{2,1,0:T(8,128)(2,1)} %bitcast.407, bf16[1024,256]{1,0:T(8,128)(2,1)} %param.16, f32[32,64]{1,0:T(8,128)S(1)} %fusion.85, f32[32,64,64]{2,1,0:T(8,128)} %copy-done.1, f32[64,64]{1,0:T(8,128)S(1)} %copy-done.8), kind=kOutput, calls=%fused_computation.36 | convolution fusion | flops 1142556672 | bytes 6316032 | tf_op jit(solution)/shard_map/uts,suc->tuc/dot_general | solution.py:38
  216.8 0.6 copy.23
  217.4 42.5 %all_to_all.24 = bf16[64,32,256]{2,1,0:T(8,128)(2,1)} all-to-all(bf16[64,32,256]{2,1,0:T(8,128)(2,1)S(1)} %copy.23), channel_id=1, replica_groups=mesh['snap'=64,'feat'=4] {'snap'}, dimensions={0} | all-to-all | bytes 2097152 | tf_op jit(solution)/shard_map/all_to_all | solution.py:76
  260.2 44.2 %all-gather.8.cloned.1.call-done = bf16[1,2048,1024]{2,1,0:T(8,128)(2,1)} async-done(((bf16[1,2048,256]{2,1,0:T(8,128)(2,1)}), bf16[1,2048,1024]{2,1,0:T(8,128)(2,1)}) %all-gather.8.cloned.1.call-update) | async-done | bytes 4194320 | tf_op jit(solution)/shard_map/all_gather | solution.py:77
  304.4 3.6 fusion.26
  308.0 6.7 %gather_fusion.1 = bf16[128,128,256]{2,1,0:T(8,128)(2,1)} fusion(bf16[1,16,128,256]{3,2,1,0:T(8,128)(2,1)S(1)} %bitcast.335, s32[128]{0:T(128)S(1)} %reshape.88), kind=kCustom, calls=%fused_computation.1 | custom fusion | bytes 16778240 | tf_op jit(solution)/shard_map/vmap()/gather | solution.py:22
  314.7 7.2 %bitcast_convert_fusion = bf16[16,256,128]{1,2,0:T(8,128)(2,1)} fusion(bf16[16,8,128,256]{3,2,1,0:T(8,128)(2,1)} %bitcast.336, bf16[1,16,8,128,128]{4,3,2,1,0:T(8,128)(2,1)} %param.12), kind=kOutput, calls=%fused_computation.27 | convolution fusion | flops 1074266112 | bytes 13631488 | tf_op jit(solution)/shard_map/srkij,srkjc->sric/dot_general | solution.py:23
  321.9 49.5 %all-gather.10.cloned.1.call-done = bf16[1,2048,1024]{2,1,0:T(8,128)(2,1)} async-done(((bf16[1,2048,256]{2,1,0:T(8,128)(2,1)}), bf16[1,2048,1024]{2,1,0:T(8,128)(2,1)}) %all-gather.10.cloned.1.call-update) | async-done | bytes 4194320 | tf_op jit(solution)/shard_map/all_gather | solution.py:80
  371.4 4.4 %fusion.35 = bf16[1,2048,256]{2,1,0:T(8,128)(2,1)} fusion(bf16[1024,256]{1,0:T(8,128)(2,1)S(1)} %copy-done.7, bf16[1,2048,1024]{2,1,0:T(8,128)(2,1)} %all-gather.10.cloned.1.call-done), kind=kOutput, calls=%fused_computation.26 | convolution fusion | flops 1074790400 | bytes 5767168 | tf_op jit(solution)/shard_map/svc,cd->svd/dot_general | solution.py:30
  (94 shorter events, 2.0 us)
Async XLA Ops:
  6.5 1.2 copy-start
  6.5 68.6 %all-gather.6.cloned.1.call-start = ((), (), s32[]{:S(2)}) async-start(), calls=%async_computation.3 | async-start | bytes 5242880 | tf_op jit(solution)/shard_map/all_gather | solution.py:57
  14.5 60.6 %copy-start.4 = (bf16[1024,256]{1,0:T(8,128)(2,1)S(1)}, bf16[1024,256]{1,0:T(8,128)(2,1)}, u32[]{:S(2)}) copy-start(bf16[1024,256]{1,0:T(8,128)(2,1)} %param.13) | copy-start | bytes 1572868
  21.7 144.5 %all-gather.12.cloned.1.call-start = ((), (), s32[]{:S(2)}) async-start(), calls=%async_computation.6 | async-start | bytes 5242880 | tf_op jit(solution)/shard_map/all_gather | solution.py:63
  78.6 1.0 copy-start.2
  78.6 87.7 %copy-start.5 = (bf16[1024,256]{1,0:T(8,128)(2,1)S(1)}, bf16[1024,256]{1,0:T(8,128)(2,1)}, u32[]{:S(2)}) copy-start(bf16[1024,256]{1,0:T(8,128)(2,1)} %param.14) | copy-start | bytes 1572868
  119.2 185.2 %all-gather.8.cloned.1.call-start = ((), (), s32[]{:S(2)}) async-start(), calls=%async_computation.4 | async-start | bytes 5242880 | tf_op jit(solution)/shard_map/all_gather | solution.py:77
  166.3 7.0 %copy-start.6 = (bf16[1024,256]{1,0:T(8,128)(2,1)S(1)}, bf16[1024,256]{1,0:T(8,128)(2,1)}, u32[]{:S(2)}) copy-start(bf16[1024,256]{1,0:T(8,128)(2,1)} %param.15) | copy-start | bytes 1572868
  185.1 21.9 %copy-start.8 = (f32[64,64]{1,0:T(8,128)S(1)}, f32[64,64]{1,0:T(8,128)}, u32[]{:S(2)}) copy-start(f32[64,64]{1,0:T(8,128)} %param.19) | copy-start | bytes 49156
  206.0 1.0 copy-start.1
  216.8 87.6 %copy-start.3 = (bf16[2048,256]{1,0:T(8,128)(2,1)S(1)}, bf16[2048,256]{1,0:T(8,128)(2,1)}, u32[]{:S(2)}) copy-start(bf16[2048,256]{1,0:T(8,128)(2,1)} %copy-done.2) | copy-start | bytes 3145732
  259.9 111.5 %all-gather.10.cloned.1.call-start = ((), (), s32[]{:S(2)}) async-start(), calls=%async_computation.5 | async-start | bytes 5242880 | tf_op jit(solution)/shard_map/all_gather | solution.py:80
  314.7 56.7 %copy-start.7 = (bf16[1024,256]{1,0:T(8,128)(2,1)S(1)}, bf16[1024,256]{1,0:T(8,128)(2,1)}, u32[]{:S(2)}) copy-start(bf16[1024,256]{1,0:T(8,128)(2,1)} %param.18) | copy-start | bytes 1572868
Sparse Core Ops, SparseCore 0:
  21.8 53.2 all-gather.5
  119.3 46.8 all-gather.11
  260.0 44.2 all-gather.7
  322.1 49.3 all-gather.9
